TPU v7x, 32 devices: a whole 2x2x4 slice. The times are simulated.
32 devices in a mesh: groups: 2 (over y), latent: 8 (over z, x), hidden: 2 (over core).
Axes of the slice: x: 2, y: 2, z: 4, core: 2. Of those that a mesh axis runs over, the one named last changes fastest.
Arguments:
- input_codes: int32 [288, 2304], P('groups', ('latent', 'hidden')), parts along dimension 0, may hold values from -128 to 127
- cotangent_codes: int32 [288, 2304], P('groups', ('latent', 'hidden')), parts along dimension 0, may hold values from -128 to 127
- dictionary: bfloat16 [8192, 2304], P(('latent', 'hidden')), as said below
- encoder_bias: float32 [8192], P(('latent', 'hidden')), may hold values from -12 to 0, as said below
- decoder_bias: float32 [2304], replicated, may hold values from -1.2 to 1.2
- norm_gain: float32 [2304], replicated, may hold values from 0.1 to 1.9
- gate_weight: bfloat16 [8192, 2304], P(('latent', 'hidden')), may hold values from -0.1875 to 0.1875
- up_weight: bfloat16 [8192, 2304], P(('latent', 'hidden')), may hold values from -0.1875 to 0.1875
- down_weight: bfloat16 [8192, 2304], P(('latent', 'hidden')), may hold values from -0.09375 to 0.09375
Outputs:
- block_output: bfloat16 [288, 2304], P('groups', ('latent', 'hidden')), parts along dimension 0
- dictionary_grad: bfloat16 [8192, 4608], P(('latent', 'hidden'), 'groups'), parts along dimension 1
There are 2 independent parts, one for each index of `groups`. A program takes and returns all parts, laid end to end along the dimension named above; an argument that names none is the same for every part. Nothing has to cross between parts.
Inputs may be any that keep to these rules, and one draw needn't show every extreme that they name: `dictionary`: every entry is a whole multiple of 2^-10, at most 119 such units in magnitude. `encoder_bias`: every entry is a whole multiple of 2^-16.
All inputs are finite; a program needn't handle non-finite values.
Results may differ from a plain program's by a relative error of at most 0.0072.
Values may be sent and summed in bfloat16 or wider, within the bound.
A program may use at most 64 MiB of HBM per device.

v0:
```python
import jax
import jax.numpy as jnp
from jax import lax
from jax.sharding import PartitionSpec as P

CODE_STEP = 2.0 ** (-6)
NORM_EPSILON = 1e-06
GELU_ROOT = 0.7978845608028654
GELU_CUBIC = 0.044715
ACROSS = (((1,), (1,)), ((), ()))
DOWNWARD = (((0,), (0,)), ((), ()))


def gelu_parts(values):
    argument = GELU_ROOT * (values + GELU_CUBIC * values * values * values)
    tanh_value = jnp.tanh(argument)
    result = 0.5 * values * (1.0 + tanh_value)
    derivative = 0.5 * (1.0 + tanh_value) + 0.5 * values * (
        1.0 - tanh_value * tanh_value
    ) * GELU_ROOT * (1.0 + 3.0 * GELU_CUBIC * values * values)
    return (result, derivative)


def per_device(
    input_codes,
    cotangent_codes,
    dictionary,
    encoder_bias,
    decoder_bias,
    norm_gain,
    gate_weight,
    up_weight,
    down_weight,
):
    own_width = input_codes.shape[1]
    model_width = own_width * lax.axis_size(("latent", "hidden"))
    cotangent_local = (cotangent_codes.astype(jnp.float32) * CODE_STEP).astype(jnp.bfloat16)
    hidden_grad = None
    inputs_local = (input_codes.astype(jnp.float32) * CODE_STEP).astype(jnp.bfloat16)
    inputs = lax.all_gather(inputs_local, ("latent", "hidden"), axis=1, tiled=True)
    preact = (
        lax.dot_general(inputs, dictionary, ACROSS, preferred_element_type=jnp.float32)
        + encoder_bias
    )
    latents = jnp.maximum(preact, 0.0).astype(jnp.bfloat16)
    partial_value = jnp.dot(latents, dictionary, preferred_element_type=jnp.float32)
    rebuilt = lax.psum(partial_value, ("latent", "hidden")) + decoder_bias
    inverse = lax.rsqrt(
        jnp.sum(rebuilt * rebuilt, axis=1, keepdims=True) / model_width + NORM_EPSILON
    )
    normed = (rebuilt * inverse * norm_gain).astype(jnp.bfloat16)
    target = inputs.astype(jnp.float32)
    gate_proj = lax.dot_general(normed, gate_weight, ACROSS, preferred_element_type=jnp.float32)
    up_proj = lax.dot_general(normed, up_weight, ACROSS, preferred_element_type=jnp.float32)
    gelu_value, gelu_slope = gelu_parts(gate_proj)
    hidden = (gelu_value * up_proj).astype(jnp.bfloat16)
    output_terms = jnp.dot(hidden, down_weight, preferred_element_type=jnp.float32)
    block_output = lax.psum_scatter(
        output_terms, ("latent", "hidden"), scatter_dimension=1, tiled=True
    ).astype(jnp.bfloat16)
    hidden_grad = lax.dot_general(
        lax.all_gather(cotangent_local, ("latent", "hidden"), axis=1, tiled=True),
        down_weight,
        ACROSS,
        preferred_element_type=jnp.float32,
    )
    gate_grad = (hidden_grad * up_proj * gelu_slope).astype(jnp.bfloat16)
    up_grad = (hidden_grad * gelu_value).astype(jnp.bfloat16)
    partial_grad = jnp.dot(gate_grad, gate_weight, preferred_element_type=jnp.float32) + jnp.dot(
        up_grad, up_weight, preferred_element_type=jnp.float32
    )
    scaled = lax.psum(partial_grad, ("latent", "hidden")) * norm_gain
    inner_row = jnp.sum(scaled * rebuilt, axis=1, keepdims=True)
    inverse_cube = inverse * inverse * inverse
    rebuilt_grad = (
        inverse * scaled - inverse_cube * rebuilt * (inner_row / model_width) + (rebuilt - target)
    ).astype(jnp.bfloat16)
    latent_grad = lax.dot_general(
        rebuilt_grad, dictionary, ACROSS, preferred_element_type=jnp.float32
    )
    preact_grad = jnp.where(preact > 0.0, latent_grad, 0.0).astype(jnp.bfloat16)
    dictionary_grad = lax.dot_general(
        latents, rebuilt_grad, DOWNWARD, preferred_element_type=jnp.float32
    ) + lax.dot_general(preact_grad, inputs, DOWNWARD, preferred_element_type=jnp.float32)
    return (block_output, dictionary_grad.astype(jnp.bfloat16))


def solution(mesh):
    in_specs = (
        P("groups", ("latent", "hidden")),
        P("groups", ("latent", "hidden")),
        P(("latent", "hidden"), None),
        P(("latent", "hidden")),
        P(),
        P(),
        P(("latent", "hidden"), None),
        P(("latent", "hidden"), None),
        P(("latent", "hidden"), None),
    )
    out_specs = (P("groups", ("latent", "hidden")), P(("latent", "hidden"), "groups"))
    return jax.shard_map(
        per_device, mesh=mesh, in_specs=in_specs, out_specs=out_specs, check_vma=False
    )
```

profile of v0, /device:TPU:0, one launch (start us, length us, event | category | flops | bytes accessed | tf_op | source)
XLA Modules:
  0.0 309.8 jit_solution(10657653489420089251)
XLA Ops:
  7.2 1.2 copy.11
  8.4 26.4 %all_gather.6 = bf16[144,2304]{0,1:T(8,128)(2,1)S(1)} all-gather(bf16[144,144]{0,1:T(8,128)(2,1)S(1)} %multiply_convert_fusion.6), channel_id=1, replica_groups=mesh['groups'=2,'latent'=8,'hidden'=2] {'latent','hidden'}, dimensions={1}, use_global_device_ids=true | all-gather | bytes 705024 | tf_op jit(solution)/shard_map/all_gather | solution.py:40
  34.8 0.9 convolution_add_fusion.2
  35.8 0.7 copy-done.8
  36.5 1.6 fusion.19
  38.1 1.7 copy.12
  39.8 0.9 multiply_convert_fusion.5
  40.7 24.5 %all_gather.7 = bf16[144,2304]{0,1:T(8,128)(2,1)S(1)} all-gather(bf16[144,144]{0,1:T(8,128)(2,1)S(1)} %multiply_convert_fusion.5), channel_id=1, replica_groups=mesh['groups'=2,'latent'=8,'hidden'=2] {'latent','hidden'}, dimensions={1}, use_global_device_ids=true | all-gather | bytes 705024 | tf_op jit(solution)/shard_map/all_gather | solution.py:62
  65.3 3.4 %fusion.38 = f32[144,512]{1,0:T(8,128)} fusion(bf16[144,2304]{0,1:T(8,128)(2,1)S(1)} %all_gather.7, bf16[512,2304]{1,0:T(8,128)(2,1)} %param.17), kind=kOutput, calls=%fused_computation.57 | convolution fusion | flops 339738624 | bytes 3317760 | tf_op jit(solution)/shard_map/dot_general | solution.py:61
  68.6 63.1 %all-reduce.3.cloned.1.call-done = f32[144,2304]{1,0:T(8,128)} async-done(((f32[144,2304]{1,0:T(8,128)}), f32[144,2304]{1,0:T(8,128)}) %all-reduce.3.cloned.1.call-update) | async-done | bytes 1327120 | tf_op jit(solution)/shard_map/psum | solution.py:47
  131.7 1.6 multiply_reduce_fusion.1
  133.9 2.8 fusion.37
  136.7 0.9 fusion.36
  137.7 0.8 copy-done.3
  139.2 1.7 convolution_add_fusion.1
  141.0 1.3 copy.13
  142.2 4.4 %convolution_bitcast_fusion = f32[2304,144]{1,0:T(8,128)} fusion(bf16[512,2304]{1,0:T(8,128)(2,1)} %param.17, f32[144,512]{1,0:T(8,128)} %copy-done.7, f32[144,512]{1,0:T(8,128)} %copy-done.5), kind=kOutput, calls=%fused_computation.2 | convolution fusion | flops 340475904 | bytes 4276224
  146.6 88.4 %all-reduce.5.cloned.1.call-done = f32[144,2304]{1,0:T(8,128)} async-done(((f32[144,2304]{1,0:T(8,128)}), f32[144,2304]{1,0:T(8,128)}) %all-reduce.5.cloned.1.call-update) | async-done | bytes 1327120 | tf_op jit(solution)/shard_map/psum | solution.py:72
  235.0 2.1 multiply_reduce_fusion
  237.5 2.5 add_convert_fusion
  240.0 5.1 %fusion.2 = f32[512,2304]{1,0:T(8,128)} fusion(bf16[144,2304]{0,1:T(8,128)(2,1)S(1)} %all_gather.6, bf16[144,2304]{1,0:T(8,128)(2,1)} %add_convert_fusion, bf16[512,2304]{1,0:T(8,128)(2,1)S(1)} %copy-done, f32[144,512]{1,0:T(8,128)} %copy-done.8), kind=kOutput, calls=%fused_computation.11 | convolution fusion | flops 679698432 | bytes 8699904 | tf_op jit(solution)/shard_map/dot_general | solution.py:84
  245.1 5.1 %fusion = bf16[512,2304]{1,0:T(8,128)(2,1)} fusion(f32[512,2304]{1,0:T(8,128)} %fusion.2, bf16[144,2304]{1,0:T(8,128)(2,1)} %add_convert_fusion, f32[144,512]{1,0:T(8,128)} %copy-done.8), kind=kOutput, calls=%fused_computation.1 | convolution fusion | flops 342245376 | bytes 8036352 | tf_op jit(solution)/shard_map/dot_general | solution.py:82
  250.2 51.5 %reduce-scatter.4.cloned.1.call-done = f32[144,144]{1,0:T(8,128)} async-done(((f32[2304,144]{1,0:T(8,128)}), f32[144,144]{1,0:T(8,128)}) %reduce-scatter.4.cloned.1.call-update) | async-done | bytes 82960
  301.7 1.6 copy.15
  (38 shorter events, 1.9 us)
Async XLA Ops:
  7.2 27.7 %copy-start = (bf16[512,2304]{1,0:T(8,128)(2,1)S(1)}, bf16[512,2304]{1,0:T(8,128)(2,1)}, u32[]{:S(2)}) copy-start(bf16[512,2304]{1,0:T(8,128)(2,1)} %param.11) | copy-start | bytes 7077892
  7.2 27.7 %copy-start.14 = (f32[512]{0:T(512)S(1)}, f32[512]{0:T(512)}, u32[]{:S(2)}) copy-start(f32[512]{0:T(512)} %param.12) | copy-start | bytes 6148
  7.2 124.5 %all-reduce.3.cloned.1.call-start = ((), (), s32[]{:S(2)}) async-start(), calls=%async_computation.1 | async-start | bytes 2654208 | tf_op jit(solution)/shard_map/psum | solution.py:47
  35.8 0.7 copy-start.8
  38.1 196.9 %all-reduce.5.cloned.1.call-start = ((), (), s32[]{:S(2)}) async-start(), calls=%async_computation.2 | async-start | bytes 2654208 | tf_op jit(solution)/shard_map/psum | solution.py:72
  65.3 66.4 %copy-start.10 = (f32[2304]{0:T(1024)S(1)}, f32[2304]{0:T(1024)}, u32[]{:S(2)}) copy-start(f32[2304]{0:T(1024)} %param.13) | copy-start | bytes 27652
  131.7 2.2 copy-start.1
  131.7 2.2 copy-start.11
  133.9 2.8 copy-start.4
  136.7 2.5 copy-start.5
  136.7 1.8 copy-start.3
  136.7 1.8 copy-start.9
  138.5 0.7 copy-start.7
  140.9 160.8 %reduce-scatter.4.cloned.1.call-start = ((), (), s32[]{:S(2)}) async-start(), calls=%async_computation.3 | async-start | bytes 2506752
  235.0 2.2 copy-start.2
  235.0 2.5 copy-start.6
  235.0 2.5 copy-start.12
  235.0 2.5 copy-start.13
Sparse Core Ops, SparseCore 0:
  38.2 93.4 all-reduce.2
  141.0 93.9 all-reduce.4
  238.7 62.8 reduce-scatter.3
where the time goes:
time: 310 us
  waiting for transfers between devices  203 us (65%)
  blocking collectives  50.9 us (16%)
  matrix products  26.4 us (9%)
  between operations  13.9 us (4%)
  other arithmetic  7.82 us (3%)
  local copies, waits for them, and re-layouts  7.76 us (3%)
    psum x1, waiting for transfers between devices, per_device(): scaled = lax.psum(partial_grad, ('latent', 'hidden')) * norm_gain  88.4 us
    psum x1, waiting for transfers between devices, per_device(): rebuilt = lax.psum(partial_value, ('latent', 'hidden')) + decoder_bias  63.1 us
    unnamed x4, waiting for transfers between devices  51.5 us
    all_gather x1, blocking collectives, per_device(): lax.all_gather(inputs_local, ('latent', 'hidden'), axis=1, tiled=True)  26.4 us
    all_gather x1, blocking collectives, per_device(): lax.all_gather(cotangent_local, ('latent', 'hidden'), axis=1, tiled=True)  24.5 us
    unnamed x33, local copies, waits for them, and re-layouts  6.49 us
  transfers between devices with their start and end apart: 3, of which 3 were waited for; matrix products, arithmetic and copies ran while one was open for 9% of the time, Pallas kernels for 0%

commit v1 on v0

--- a/solution.py
+++ b/solution.py
@@ -37,7 +37,15 @@
     cotangent_local = (cotangent_codes.astype(jnp.float32) * CODE_STEP).astype(jnp.bfloat16)
     hidden_grad = None
     inputs_local = (input_codes.astype(jnp.float32) * CODE_STEP).astype(jnp.bfloat16)
-    inputs = lax.all_gather(inputs_local, ("latent", "hidden"), axis=1, tiled=True)
+    inputs = jnp.concatenate(
+        lax.all_to_all(
+            jnp.stack([inputs_local] * lax.axis_size(("latent", "hidden"))),
+            ("latent", "hidden"),
+            0,
+            0,
+        ),
+        axis=1,
+    )
     preact = (
         lax.dot_general(inputs, dictionary, ACROSS, preferred_element_type=jnp.float32)
         + encoder_bias

time: 310 us -> 328 us (1.058)
  waiting for transfers between devices: 203 us -> 235 us
  blocking collectives: 50.9 us -> 29.6 us
  starting transfers between devices: 0.12 us -> 7.69 us
  local copies, waits for them, and re-layouts: 7.76 us -> 12.1 us
  other arithmetic: 7.82 us -> 4.39 us
    all_gather x1 -> x0, blocking collectives: 26.4 us -> none  [per_device(): lax.all_gather(inputs_local, ('latent', 'hidden'), axis=1, tiled=True)]
    all_to_all x0 -> x1, waiting for transfers between devices: none -> 24.9 us  [per_device(): lax.all_to_all(jnp.stack([inputs_local] * lax.axis_size(('latent', 'hidde...]
    all_to_all x0 -> x1, starting transfers between devices: none -> 7.56 us  [per_device(): lax.all_to_all(jnp.stack([inputs_local] * lax.axis_size(('latent', 'hidde...]
    reshape x0 -> x2, local copies, waits for them, and re-layouts: none -> 5.28 us  [per_device(): jnp.concatenate(lax.all_to_all(jnp.stack([inputs_local] * lax.axis_size((...]
    all_gather x1, blocking collectives: 24.5 us -> 29.6 us  [per_device(): lax.all_gather(cotangent_local, ('latent', 'hidden'), axis=1, tiled=True)]
  transfers between devices with their start and end apart: 3 -> 4, of which waited for: 3 -> 4; matrix products, arithmetic and copies ran while one was open for 9% -> 6% of each run, Pallas kernels for 0% -> 0%
where the time goes in v1:
time: 328 us; the launch traced here: 327 us
  waiting for transfers between devices  235 us (72%)
  blocking collectives  29.6 us (9%)
  matrix products  25 us (8%)
  between operations  13.9 us (4%)
  local copies, waits for them, and re-layouts  12.1 us (4%)
  starting transfers between devices  7.69 us (2%)
  other arithmetic  4.39 us (1%)
    psum x1, waiting for transfers between devices, per_device(): scaled = lax.psum(partial_grad, ('latent', 'hidden')) * norm_gain  89.7 us
    psum x1, waiting for transfers between devices, per_device(): rebuilt = lax.psum(partial_value, ('latent', 'hidden')) + decoder_bias  65.9 us
    unnamed x4, waiting for transfers between devices  54 us
    all_gather x1, blocking collectives, per_device(): lax.all_gather(cotangent_local, ('latent', 'hidden'), axis=1, tiled=True)  29.6 us
    all_to_all x1, waiting for transfers between devices, per_device(): lax.all_to_all(jnp.stack([inputs_local] * lax.axis_size(('latent', 'hidde...  24.9 us
    all_to_all x1, starting transfers between devices, per_device(): lax.all_to_all(jnp.stack([inputs_local] * lax.axis_size(('latent', 'hidde...  7.56 us
  transfers between devices with their start and end apart: 4, of which 4 were waited for; matrix products, arithmetic and copies ran while one was open for 6% of the time, Pallas kernels for 0%

profile of v1, /device:TPU:0, one launch (start us, length us, event | category | flops | bytes accessed | tf_op | source)
XLA Modules:
  0.0 327.3 jit_solution(11567296062709470050)
XLA Ops:
  7.2 1.2 copy.11
  8.5 1.1 stack.2
  9.6 7.6 %all-to-all-start = ((bf16[16,144,144]{2,1,0:T(8,128)(2,1)}), bf16[16,144,144]{2,1,0:T(8,128)(2,1)}, u32[]{:S(2)}, u32[]{:S(2)}) async-start(bf16[16,144,144]{2,1,0:T(8,128)(2,1)} %stack.2), calls=%async_computation | async-start | bytes 2359296 | tf_op jit(solution)/shard_map/all_to_all | solution.py:41
  17.3 24.9 %all-to-all-done = bf16[16,144,144]{2,1,0:T(8,128)(2,1)} async-done(((bf16[16,144,144]{2,1,0:T(8,128)(2,1)}), bf16[16,144,144]{2,1,0:T(8,128)(2,1)}, u32[]{:S(2)}, u32[]{:S(2)}) %all-to-all-start) | async-done | bytes 663584 | tf_op jit(solution)/shard_map/all_to_all | solution.py:41
  42.2 2.7 copy.13
  44.9 2.6 reshape.34
  47.5 0.9 convolution_add_fusion.2
  48.5 0.7 copy-done.6
  49.2 1.6 fusion.19
  50.9 29.6 %all_gather.3 = bf16[144,2304]{0,1:T(8,128)(2,1)S(1)} all-gather(bf16[144,144]{0,1:T(8,128)(2,1)S(1)} %multiply_convert_fusion.5), channel_id=1, replica_groups=mesh['groups'=2,'latent'=8,'hidden'=2] {'latent','hidden'}, dimensions={1}, use_global_device_ids=true | all-gather | bytes 705024 | tf_op jit(solution)/shard_map/all_gather | solution.py:70
  80.5 3.4 %fusion.38 = f32[144,512]{1,0:T(8,128)} fusion(bf16[144,2304]{0,1:T(8,128)(2,1)S(1)} %all_gather.3, bf16[512,2304]{1,0:T(8,128)(2,1)} %param.17), kind=kOutput, calls=%fused_computation.57 | convolution fusion | flops 339738624 | bytes 3317760 | tf_op jit(solution)/shard_map/dot_general | solution.py:69
  83.9 65.9 %all-reduce.3.cloned.1.call-done = f32[144,2304]{1,0:T(8,128)} async-done(((f32[144,2304]{1,0:T(8,128)}), f32[144,2304]{1,0:T(8,128)}) %all-reduce.3.cloned.1.call-update) | async-done | bytes 1327120 | tf_op jit(solution)/shard_map/psum | solution.py:55
  149.8 1.6 multiply_reduce_fusion.1
  151.6 2.7 fusion.37
  154.3 0.9 fusion.36
  156.7 1.7 convolution_add_fusion.1
  158.5 4.3 %convolution_bitcast_fusion = f32[2304,144]{1,0:T(8,128)} fusion(bf16[512,2304]{1,0:T(8,128)(2,1)} %param.17, f32[144,512]{1,0:T(8,128)} %copy-done.9, f32[144,512]{1,0:T(8,128)S(1)} %fusion.37), kind=kOutput, calls=%fused_computation.2 | convolution fusion | flops 340475904 | bytes 4276224
  162.8 89.7 %all-reduce.5.cloned.1.call-done = f32[144,2304]{1,0:T(8,128)} async-done(((f32[144,2304]{1,0:T(8,128)}), f32[144,2304]{1,0:T(8,128)}) %all-reduce.5.cloned.1.call-update) | async-done | bytes 1327120 | tf_op jit(solution)/shard_map/psum | solution.py:80
  252.5 2.2 multiply_reduce_fusion
  255.5 0.8 copy-done.5
  256.4 3.0 fusion.18
  259.3 5.8 %fusion = bf16[512,2304]{1,0:T(8,128)(2,1)} fusion(f32[512,2304]{1,0:T(8,128)} %fusion.18, bf16[144,2304]{1,0:T(8,128)(2,1)S(1)} %reshape.34, bf16[144,2304]{1,0:T(8,128)(2,1)} %copy-done.5, bf16[512,2304]{1,0:T(8,128)(2,1)S(1)} %copy-done, f32[144,512]{1,0:T(8,128)S(1)} %copy-done.7), kind=kOutput, calls=%fused_computation.1 | convolution fusion | flops 682057728 | bytes 11059200 | tf_op jit(solution)/shard_map/dot_general | solution.py:92
  265.2 54.0 %reduce-scatter.4.cloned.1.call-done = f32[144,144]{1,0:T(8,128)} async-done(((f32[2304,144]{1,0:T(8,128)}), f32[144,144]{1,0:T(8,128)}) %reduce-scatter.4.cloned.1.call-update) | async-done | bytes 82960
  319.2 1.6 copy.16
  (42 shorter events, 2.8 us)
Async XLA Ops:
  7.2 40.4 %copy-start = (bf16[512,2304]{1,0:T(8,128)(2,1)S(1)}, bf16[512,2304]{1,0:T(8,128)(2,1)}, u32[]{:S(2)}) copy-start(bf16[512,2304]{1,0:T(8,128)(2,1)} %param.11) | copy-start | bytes 7077892
  9.6 7.6 %copy-start.13 = (s32[144,144]{1,0:T(8,128)S(1)}, s32[144,144]{1,0:T(8,128)}, u32[]{:S(2)}) copy-start(s32[144,144]{1,0:T(8,128)} %param.10) | copy-start | bytes 248836
  9.6 32.7 %all-to-all-start = ((bf16[16,144,144]{2,1,0:T(8,128)(2,1)}), bf16[16,144,144]{2,1,0:T(8,128)(2,1)}, u32[]{:S(2)}, u32[]{:S(2)}) async-start(bf16[16,144,144]{2,1,0:T(8,128)(2,1)} %stack.2), calls=%async_computation | async-start | bytes 2359296 | tf_op jit(solution)/shard_map/all_to_all | solution.py:41
  17.1 132.7 %all-reduce.3.cloned.1.call-start = ((), (), s32[]{:S(2)}) async-start(), calls=%async_computation.2 | async-start | bytes 2654208 | tf_op jit(solution)/shard_map/psum | solution.py:55
  44.9 2.6 copy-start.14
  48.5 0.7 copy-start.6
  50.8 201.7 %all-reduce.5.cloned.1.call-start = ((), (), s32[]{:S(2)}) async-start(), calls=%async_computation.3 | async-start | bytes 2654208 | tf_op jit(solution)/shard_map/psum | solution.py:80
  80.5 69.3 %copy-start.11 = (f32[2304]{0:T(1024)S(1)}, f32[2304]{0:T(1024)}, u32[]{:S(2)}) copy-start(f32[2304]{0:T(1024)} %param.13) | copy-start | bytes 27652
  83.9 67.6 %copy-start.12 = (f32[2304]{0:T(1024)S(1)}, f32[2304]{0:T(1024)}, u32[]{:S(2)}) copy-start(f32[2304]{0:T(1024)} %param.14) | copy-start | bytes 27652
  149.8 1.7 copy-start.1
  151.6 2.7 copy-start.4
  154.3 1.7 copy-start.3
  154.3 1.7 copy-start.10
  156.0 0.7 copy-start.9
  158.4 160.7 %reduce-scatter.4.cloned.1.call-start = ((), (), s32[]{:S(2)}) async-start(), calls=%async_computation.4 | async-start | bytes 2506752
  252.5 2.2 copy-start.2
  252.5 2.5 copy-start.8
  255.0 1.4 copy-start.7
  255.5 0.8 copy-start.5
Sparse Core Ops, SparseCore 0:
  50.9 98.8 all-reduce.2
  158.5 93.8 all-reduce.4
  256.2 62.8 reduce-scatter.3
